TPU v7x, 32 devices: a whole 2x2x4 slice. The times are simulated.
32 devices in a mesh: grp: 2 (over y), wide: 8 (over z, x), tm: 2 (over core).
Axes of the slice: x: 2, y: 2, z: 4, core: 2. Of those that a mesh axis runs over, the one named last changes fastest.
Arguments:
- voltages: bfloat16 [2048, 65536], P('wide', ('grp', 'tm')), parts along dimension 1, may hold values from -6 to 6
- channels: int32 [16], replicated, may hold values from 0 to 1023, as said below
- tile_pairs: int32 [128, 2], replicated, may hold values from 0 to 31, as said below
Outputs:
- visibility: bfloat16 [32, 128, 64, 128], P(('grp', 'wide', 'tm')), parts along dimension 0
There are 2 independent parts, one for each index of `grp`. A program takes and returns all parts, laid end to end along the dimension named above; an argument that names none is the same for every part. Nothing has to cross between parts.
Inputs may be any that keep to these rules, and one draw needn't show every extreme that they name: `channels`: 16 different channel numbers in no fixed order; 0 and 1023 are always among them. `tile_pairs`: 128 different ordered tile pairs; (0, 0) and (31, 31) are always among them.
All inputs are finite; a program needn't handle non-finite values.
Results may differ from a plain program's by a relative error of at most 0.0071.
Values may be sent and summed in bfloat16 or wider, within the bound.
A program may use at most 64 MiB of HBM per device.

v0:
```python
import jax
import jax.numpy as jnp
from jax import lax
from jax.sharding import PartitionSpec as P

TILE = 64
NFFT = 2048


def dft_table(channels, length):
    samples = jnp.arange(length, dtype=jnp.int32)
    phase = channels[:, None] * samples[None, :] % length
    angle = 2.0 * jnp.pi / length * phase.astype(jnp.float32)
    window = 0.5 - 0.5 * jnp.cos(2.0 * jnp.pi / length * samples.astype(jnp.float32))
    scale = 1.0 / jnp.sqrt(jnp.float32(0.375 * length))
    table = jnp.concatenate([window * jnp.cos(angle), -window * jnp.sin(angle)], 0) * scale
    return table.astype(jnp.bfloat16)


def corner_turn(spectrum):
    return lax.all_to_all(
        lax.all_to_all(spectrum, "wide", split_axis=1, concat_axis=2, tiled=True),
        "tm",
        split_axis=1,
        concat_axis=3,
        tiled=True,
    )


def shards(voltages, channels, tile_pairs):
    n_wide = lax.axis_size("wide")
    n_time = lax.axis_size("tm")
    in_dev = voltages.shape[0]
    frames_dev = voltages.shape[1] // NFFT
    count = channels.shape[0]
    per_dev = count // (n_wide * n_time)
    npairs = tile_pairs.shape[0]
    table = dft_table(channels, NFFT)

    def spectrum(start, frames):
        block = voltages.reshape(in_dev * frames, NFFT)
        result = lax.dot_general(
            table, block, (((1,), (1,)), ((), ())), preferred_element_type=jnp.float32
        )
        return result.astype(jnp.bfloat16).reshape(2, count, in_dev, frames)

    turned = corner_turn(spectrum(0, frames_dev))
    frames = turned.shape[3]
    tiles_all = turned.shape[2] // TILE
    tiled = turned.reshape(2, per_dev, tiles_all, TILE, frames)

    def stacked(which):
        picked = jnp.take(tiled, tile_pairs[:, which], axis=2)
        return picked.transpose(2, 1, 0, 3, 4).reshape(npairs, per_dev, 2 * TILE, frames)

    first = stacked(0)
    second = stacked(1)
    sums = jnp.einsum("pcif,pcjf->pcij", first, second, preferred_element_type=jnp.float32)
    frames_all = frames_dev * n_time
    real = sums[:, :, :TILE, :TILE] + sums[:, :, TILE:, TILE:]
    imag = sums[:, :, :TILE, TILE:] - sums[:, :, TILE:, :TILE]
    visibility = (jnp.concatenate([real, imag], 3) / frames_all).astype(jnp.bfloat16)
    return visibility.transpose(1, 0, 2, 3)


def solution(mesh):
    return jax.shard_map(
        shards,
        mesh=mesh,
        in_specs=(P("wide", ("grp", "tm")), P(), P()),
        out_specs=P(("grp", "wide", "tm"), None, None, None),
        check_vma=False,
    )
```

profile of v0, /device:TPU:0, one launch (start us, length us, event | category | flops | bytes accessed | tf_op | source)
XLA Modules:
  0.0 67.3 jit_solution(2652461978201646500)
XLA Ops:
  0.0 0.1 multiply_subtract_fusion
  0.1 0.0 copy-start.1
  0.1 13.5 %reshape.88 = bf16[2048,2048]{1,0:T(8,128)(2,1)} reshape(bf16[256,16384]{1,0:T(8,128)(2,1)} %param.5) | data formatting | bytes 16777216 | tf_op jit(solution)/shard_map/reshape | solution.py:41
  13.6 0.0 copy-done.1
  13.6 0.6 cosine_multiply_fusion
  14.2 0.0 copy-start
  14.2 6.0 %convolution_convert_fusion = bf16[32,2048]{1,0:T(8,128)(2,1)S(1)} fusion(bf16[2048,2048]{1,0:T(8,128)(2,1)} %reshape.88, f32[16,2048]{1,0:T(8,128)S(1)} %get-tuple-element.15, f32[16,2048]{1,0:T(8,128)S(1)} %get-tuple-element.14), kind=kOutput, calls=%fused_computation.9 | convolution fusion | flops 268697600 | bytes 8781824 | tf_op jit(solution)/shard_map/dot_general | solution.py:42
  20.2 0.3 copy.21
  20.5 0.4 reshape.89
  20.9 1.6 %copy.22 = bf16[2,16,256,8]{2,3,0,1:T(8,128)(2,1)} copy(bf16[2,16,256,8]{1,0,3,2:T(2,128)(2,1)S(1)} %reshape.89) | data formatting | bytes 262144 | tf_op jit(solution)/shard_map/reshape | solution.py:45
  22.5 7.3 %all-to-all-start = ((bf16[2,16,256,8]{2,3,0,1:T(8,128)(2,1)}), bf16[2,16,256,8]{2,3,0,1:T(8,128)(2,1)S(1)}, u32[]{:S(2)}, u32[]{:S(2)}) async-start(bf16[2,16,256,8]{2,3,0,1:T(8,128)(2,1)} %copy.22), calls=%async_computation | async-start | bytes 262144 | tf_op jit(solution)/shard_map/all_to_all | solution.py:22
  29.8 0.0 copy-done
  29.8 7.3 %all-to-all-done = bf16[2,16,256,8]{2,3,0,1:T(8,128)(2,1)S(1)} async-done(((bf16[2,16,256,8]{2,3,0,1:T(8,128)(2,1)}), bf16[2,16,256,8]{2,3,0,1:T(8,128)(2,1)S(1)}, u32[]{:S(2)}, u32[]{:S(2)}) %all-to-all-start) | async-done | bytes 131104 | tf_op jit(solution)/shard_map/all_to_all | solution.py:22
  37.1 3.8 %all_to_all.33 = bf16[2,2,2048,8]{2,3,0,1:T(8,128)(2,1)S(1)} all-to-all(bf16[2,2,2048,8]{2,3,0,1:T(8,128)(2,1)S(1)} %copy.25), channel_id=1, replica_groups=mesh['grp'=2,'wide'=8,'tm'=2] {'tm'}, dimensions={1} | all-to-all | bytes 262144 | tf_op jit(solution)/shard_map/all_to_all | solution.py:21
  41.0 0.2 reshape.90
  41.2 0.1 copy.35
  41.3 0.8 %gather_fusion.1 = bf16[128,2,64,16]{2,3,1,0:T(8,128)(2,1)S(1)} fusion(bf16[2,32,64,16]{2,3,1,0:T(8,128)(2,1)S(1)} %bitcast.50, s32[1024]{0:T(1024)S(1)} %get-tuple-element.18), kind=kCustom, calls=%fused_computation.1.clone | custom fusion | bytes 1049088 | tf_op jit(solution)/shard_map/jit(_take)/gather | solution.py:53
  42.2 0.2 fusion.3
  42.4 1.4 %copy.30 = bf16[128,1,2,64,16]{0,4,3,2,1:T(8,128)(2,1)S(1)} copy(bf16[128,1,2,64,16]{3,4,2,0,1:T(8,128)(2,1)S(1)} %fusion.3) | data formatting | bytes 1048576 | tf_op jit(solution)/shard_map/transpose | solution.py:54
  43.8 0.7 %copy.32 = bf16[128,128,16]{1,2,0:T(8,128)(2,1)S(1)} copy(bf16[128,128,16]{0,2,1:T(8,128)(2,1)S(1)} %bitcast.52) | data formatting | bytes 1048576 | tf_op jit(solution)/shard_map/reshape.3
  44.5 0.8 %gather_fusion = bf16[128,2,64,16]{2,3,1,0:T(8,128)(2,1)S(1)} fusion(bf16[2,32,64,16]{2,3,1,0:T(8,128)(2,1)S(1)} %bitcast.51, s32[1024]{0:T(1024)S(1)} %get-tuple-element.19), kind=kCustom, calls=%fused_computation.clone | custom fusion | bytes 1049088 | tf_op jit(solution)/shard_map/jit(_take)/gather | solution.py:53
  45.4 0.2 fusion.4
  45.6 1.4 %copy.28 = bf16[128,1,2,64,16]{0,4,3,2,1:T(8,128)(2,1)S(1)} copy(bf16[128,1,2,64,16]{3,4,2,0,1:T(8,128)(2,1)S(1)} %fusion.4) | data formatting | bytes 1048576 | tf_op jit(solution)/shard_map/transpose | solution.py:54
  47.0 0.7 %copy.31 = bf16[128,128,16]{1,2,0:T(8,128)(2,1)S(1)} copy(bf16[128,128,16]{0,2,1:T(8,128)(2,1)S(1)} %bitcast.53) | data formatting | bytes 1048576 | tf_op jit(solution)/shard_map/reshape.2
  47.7 4.5 %convolution_bitcast_fusion = f32[128,1,128,128]{3,2,0,1:T(8,128)} fusion(bf16[128,128,16]{1,2,0:T(8,128)(2,1)S(1)} %copy.31, bf16[128,128,16]{1,2,0:T(8,128)(2,1)S(1)} %copy.32), kind=kOutput, calls=%fused_computation.8 | convolution fusion | flops 67108864 | bytes 9437184 | tf_op jit(solution)/shard_map/pcif,pcjf->pcij/dot_general | solution.py:58
  52.2 10.4 %fusion.1 = (f32[1,128,64,64]{3,2,1,0:T(8,128)S(1)}, f32[1,128,64,64]{3,2,1,0:T(8,128)}) fusion(f32[128,1,128,128]{3,2,0,1:T(8,128)} %convolution_bitcast_fusion), kind=kLoop, calls=%fused_computation.5 | loop fusion | flops 1048576 | bytes 12582912 | tf_op jit(solution)/shard_map/concatenate | solution.py:62
  62.6 4.7 %fusion.2 = bf16[1,128,64,128]{3,2,1,0:T(8,128)(2,1)} fusion(f32[1,128,64,64]{3,2,1,0:T(8,128)} %get-tuple-element.11, f32[1,128,64,64]{3,2,1,0:T(8,128)S(1)} %get-tuple-element.10), kind=kLoop, calls=%fused_computation.7 | loop fusion | flops 3145728 | bytes 6291456 | tf_op jit(solution)/shard_map/convert_element_type | solution.py:62
  (5 shorter events, 0.0 us)
Async XLA Ops:
  0.1 13.5 %copy-start.1 = (s32[16]{0:T(128)S(1)}, s32[16]{0:T(128)}, u32[]{:S(2)}) copy-start(s32[16]{0:T(128)} %param.6) | copy-start | bytes 196
  14.2 15.6 %copy-start = (s32[128,2]{0,1:T(2,128)S(1)}, s32[128,2]{0,1:T(2,128)}, u32[]{:S(2)}) copy-start(s32[128,2]{0,1:T(2,128)} %param.7) | copy-start | bytes 3076
  22.5 14.6 %all-to-all-start = ((bf16[2,16,256,8]{2,3,0,1:T(8,128)(2,1)}), bf16[2,16,256,8]{2,3,0,1:T(8,128)(2,1)S(1)}, u32[]{:S(2)}, u32[]{:S(2)}) async-start(bf16[2,16,256,8]{2,3,0,1:T(8,128)(2,1)} %copy.22), calls=%async_computation | async-start | bytes 262144 | tf_op jit(solution)/shard_map/all_to_all | solution.py:22
where the time goes:
time: 67.9 us; the launch traced here: 67.3 us
  local copies, waits for them, and re-layouts  22.1 us (33%)
  other arithmetic  16.1 us (24%)
  matrix products  10.5 us (15%)
  waiting for transfers between devices  7.31 us (11%)
  starting transfers between devices  7.28 us (11%)
  blocking collectives  3.84 us (6%)
    reshape x1, local copies, waits for them, and re-layouts, spectrum(): block = voltages.reshape(in_dev * frames, NFFT)  13.5 us
    concatenate x1, other arithmetic, shards(): jnp.concatenate([real, imag], 3) / frames_all  10.4 us
    all_to_all x1, waiting for transfers between devices, corner_turn(): lax.all_to_all(spectrum, 'wide', split_axis=1, concat_axis=2, tiled=True)  7.31 us
    all_to_all x1, starting transfers between devices, corner_turn(): lax.all_to_all(spectrum, 'wide', split_axis=1, concat_axis=2, tiled=True)  7.28 us
    dot_general x1, matrix products, spectrum(): lax.dot_general(table, block, (((1,), (1,)), ((), ())), preferred_element...  5.97 us
    convert_element_type x1, other arithmetic, shards(): (jnp.concatenate([real, imag], 3) / frames_all).astype(jnp.bfloat16)  4.66 us
    dot_general x1, matrix products, shards(): jnp.einsum('pcif,pcjf->pcij', first, second, preferred_element_type=jnp.f...  4.54 us
    all_to_all x1, blocking collectives, corner_turn(): lax.all_to_all(lax.all_to_all(spectrum, 'wide', split_axis=1, concat_axis...  3.84 us
  transfers between devices with their start and end apart: 1, of which 1 were waited for; matrix products, arithmetic and copies ran while one was open for 0% of the time, Pallas kernels for 0%

commit v1 on v0

v1 whole, which is shorter than its diff:
```python
import functools

import jax
import jax.numpy as jnp
from jax import lax
from jax.experimental import pallas as pl
from jax.experimental.pallas import tpu as pltpu
from jax.sharding import PartitionSpec as P

TILE = 64
NFFT = 2048
LANES = 128
MESH = pl.DeviceIdType.MESH


def cos_sin(multiplier, steps):
    phase = lax.rem(multiplier * steps, NFFT)
    angle = (2.0 * jnp.pi / NFFT) * phase.astype(jnp.float32)
    return jnp.cos(angle), jnp.sin(angle)


def fill_table(channels_ref, table):
    count = channels_ref.shape[0]
    highs = NFFT // LANES
    scale = 1.0 / jnp.sqrt(jnp.float32(0.375 * NFFT))
    channels = channels_ref[...]
    low = lax.broadcasted_iota(jnp.int32, (count, LANES), 1)
    low_cos, low_sin = cos_sin(channels, low)
    high_cos, high_sin = cos_sin(channels, LANES * low)
    win_low = lax.broadcasted_iota(jnp.int32, (8, LANES), 1)
    win_cos, win_sin = cos_sin(1, win_low)
    win_high_cos, win_high_sin = cos_sin(1, LANES * win_low)
    for high in range(highs):
        columns = slice(high * LANES, (high + 1) * LANES)
        wc, ws = win_high_cos[:, high : high + 1], win_high_sin[:, high : high + 1]
        window = (0.5 - 0.5 * (win_cos * wc - win_sin * ws)) * scale
        window = jnp.broadcast_to(window[:1], (count, LANES))
        hc, hs = high_cos[:, high : high + 1], high_sin[:, high : high + 1]
        real = window * (low_cos * hc - low_sin * hs)
        imag = -window * (low_sin * hc + low_cos * hs)
        table[:, columns] = jnp.concatenate([real, imag], 0).astype(jnp.bfloat16)


def transform_kernel(
    n_wide, n_tm, channels_ref, v_hbm, out, blocks, table, staged, send, in_sems, send_sems, recv_sems, own_sem
):
    frames, in_dev, _ = blocks.shape
    count = channels_ref.shape[0]
    rows = 2 * frames
    wide, tm = lax.axis_index("wide"), lax.axis_index("tm")
    me = wide * n_tm + tm
    peers = n_wide * n_tm

    loads = [
        pltpu.make_async_copy(
            v_hbm.at[:, pl.ds(f * NFFT, NFFT)], blocks.at[f], in_sems.at[f]
        )
        for f in range(frames)
    ]
    for load in loads:
        load.start()

    barrier = pltpu.get_barrier_semaphore()

    def greet(k, carry):
        peer = lax.rem(me + k, peers)
        pl.semaphore_signal(
            barrier,
            inc=1,
            device_id={"wide": peer // n_tm, "tm": lax.rem(peer, n_tm)},
            device_id_type=MESH,
        )
        return carry

    lax.fori_loop(1, peers, greet, 0)

    fill_table(channels_ref, table)

    for f in range(frames):
        loads[f].wait()
        spectrum = lax.dot_general(
            table[...], blocks[f], (((1,), (1,)), ((), ())), preferred_element_type=jnp.float32
        )
        for q in range(2):
            staged[:, q * frames + f, :] = spectrum[q * count : (q + 1) * count]
    send[...] = staged[...].astype(jnp.bfloat16)

    pl.semaphore_wait(barrier, peers - 1)
    per_dev = count // peers

    def copy_to(k):
        peer = lax.rem(me + k, peers)
        return pltpu.make_async_remote_copy(
            src_ref=send.at[pl.ds(peer * per_dev, per_dev)],
            dst_ref=out.at[wide, tm],
            send_sem=send_sems.at[k],
            recv_sem=recv_sems.at[k],
            device_id={"wide": peer // n_tm, "tm": lax.rem(peer, n_tm)},
            device_id_type=MESH,
        )

    def start(k, carry):
        copy_to(k).start()
        return carry

    def wait(k, carry):
        copy_to(k).wait()
        return carry

    lax.fori_loop(1, peers, start, 0)
    own = pltpu.make_async_copy(send.at[pl.ds(me * per_dev, per_dev)], out.at[wide, tm], own_sem)
    own.start()
    own.wait()
    lax.fori_loop(1, peers, wait, 0)


def transform(voltages, channels, n_wide, n_tm):
    in_dev, samples = voltages.shape
    frames = samples // NFFT
    count = channels.shape[0]
    peers = n_wide * n_tm
    rows = 2 * frames
    return pl.pallas_call(
        functools.partial(transform_kernel, n_wide, n_tm),
        out_shape=jax.ShapeDtypeStruct((n_wide, n_tm, count // peers, rows, in_dev), jnp.bfloat16),
        in_specs=[
            pl.BlockSpec(memory_space=pltpu.VMEM),
            pl.BlockSpec(memory_space=pltpu.HBM),
        ],
        out_specs=pl.BlockSpec(memory_space=pltpu.VMEM),
        scratch_shapes=[
            pltpu.VMEM((frames, in_dev, NFFT), jnp.bfloat16),
            pltpu.VMEM((2 * count, NFFT), jnp.bfloat16),
            pltpu.VMEM((count, rows, in_dev), jnp.float32),
            pltpu.VMEM((count, rows, in_dev), jnp.bfloat16),
            pltpu.SemaphoreType.DMA((frames,)),
            pltpu.SemaphoreType.DMA((peers,)),
            pltpu.SemaphoreType.DMA((peers,)),
            pltpu.SemaphoreType.DMA,
        ],
        compiler_params=pltpu.CompilerParams(collective_id=0, has_side_effects=True),
        name="transform",
    )(channels.reshape(count, 1), voltages)


def correlate_kernel(frames, chunk, pairs_ref, spectra, out, left, right, products, sems):
    groups, n_tm, rows, in_group = spectra.shape
    half = rows // 2
    npairs = out.shape[0]
    for g in range(groups):
        blocks = [spectra[g, t].astype(jnp.float32) for t in range(n_tm)]
        plain = jnp.concatenate(blocks, 0)
        swapped = jnp.concatenate([x for b in blocks for x in (b[half:], -b[:half])], 0)
        left[g * in_group : (g + 1) * in_group, :] = plain.T.astype(jnp.bfloat16)
        for j in range(in_group // TILE):
            columns = slice(j * TILE, (j + 1) * TILE)
            both = jnp.concatenate([plain[:, columns], swapped[:, columns]], 1)
            right[g * (in_group // TILE) + j] = both.astype(jnp.bfloat16)

    copies = []
    for c in range(npairs // chunk):
        for p in range(c * chunk, (c + 1) * chunk):
            first = left[pl.ds(pl.multiple_of(pairs_ref[0, p] * TILE, TILE), TILE), :]
            second = right[pairs_ref[1, p]]
            sums = jnp.dot(first, second, preferred_element_type=jnp.float32)
            products[p] = (sums * (1.0 / frames)).astype(jnp.bfloat16)
        span = pl.ds(c * chunk, chunk)
        copy = pltpu.make_async_copy(products.at[span], out.at[span], sems.at[c])
        copy.start()
        copies.append(copy)
    for copy in copies:
        copy.wait()


def correlate(spectra, pairs, frames):
    groups, n_tm, rows, in_group = spectra.shape
    npairs = pairs.shape[1]
    inputs = groups * in_group
    depth = n_tm * rows
    chunk = 16 if npairs % 16 == 0 else npairs
    return pl.pallas_call(
        functools.partial(correlate_kernel, frames, chunk),
        out_shape=jax.ShapeDtypeStruct((npairs, TILE, 2 * TILE), jnp.bfloat16),
        in_specs=[
            pl.BlockSpec(memory_space=pltpu.SMEM),
            pl.BlockSpec(memory_space=pltpu.VMEM),
        ],
        out_specs=pl.BlockSpec(memory_space=pltpu.HBM),
        scratch_shapes=[
            pltpu.VMEM((inputs, depth), jnp.bfloat16),
            pltpu.VMEM((inputs // TILE, depth, 2 * TILE), jnp.bfloat16),
            pltpu.VMEM((npairs, TILE, 2 * TILE), jnp.bfloat16),
            pltpu.SemaphoreType.DMA((npairs // chunk,)),
        ],
        name="correlate",
    )(pairs, spectra)


def shards(voltages, channels, tile_pairs):
    n_wide = lax.axis_size("wide")
    n_tm = lax.axis_size("tm")
    in_dev = voltages.shape[0]
    frames_all = voltages.shape[1] // NFFT * n_tm
    per_dev = channels.shape[0] // (n_wide * n_tm)
    turned = transform(voltages, channels, n_wide, n_tm)
    visibility = []
    for s in range(per_dev):
        spectra = turned[:, :, s]
        if in_dev % TILE:
            rows = spectra.shape[2]
            spectra = spectra.transpose(1, 2, 0, 3).reshape(1, n_tm, rows, n_wide * in_dev)
        visibility.append(correlate(spectra, tile_pairs.T, frames_all))
    return jnp.stack(visibility)


def solution(mesh):
    return jax.shard_map(
        shards,
        mesh=mesh,
        in_specs=(P("wide", ("grp", "tm")), P(), P()),
        out_specs=P(("grp", "wide", "tm"), None, None, None),
        check_vma=False,
    )
```

time: 67.9 us -> 20.5 us (0.30)
  local copies, waits for them, and re-layouts: 22.1 us -> 1.33 us
  Pallas kernels: 0 us -> 18.9 us
  other arithmetic: 16.1 us -> 0 us
  matrix products: 10.5 us -> 0 us
  waiting for transfers between devices: 7.31 us -> 0 us
  starting transfers between devices: 7.28 us -> 0 us
  blocking collectives: 3.84 us -> 0 us
    pallas_call x0 -> x2, Pallas kernels: none -> 18.9 us  [the longest x1 16.1 us: transform(): pl.pallas_call(functools.partial(transform_kernel, n_wide, n_tm), out_sha...]
    reshape x5 -> x1, local copies, waits for them, and re-layouts: 15.9 us -> 1.33 us  [transform(): channels.reshape(count, 1)]
    dot_general x2 -> x0, matrix products: 10.5 us -> none  [the longest x1 5.97 us: spectrum(): lax.dot_general(table, block, (((1,), (1,)), ((), ())), preferred_element...]
    concatenate x1 -> x0, other arithmetic: 10.4 us -> none  [shards(): jnp.concatenate([real, imag], 3) / frames_all]
    all_to_all x1 -> x0, waiting for transfers between devices: 7.31 us -> none  [corner_turn(): lax.all_to_all(spectrum, 'wide', split_axis=1, concat_axis=2, tiled=True)]
    all_to_all x1 -> x0, starting transfers between devices: 7.28 us -> none  [corner_turn(): lax.all_to_all(spectrum, 'wide', split_axis=1, concat_axis=2, tiled=True)]
    convert_element_type x1 -> x0, other arithmetic: 4.66 us -> none  [shards(): (jnp.concatenate([real, imag], 3) / frames_all).astype(jnp.bfloat16)]
    all_to_all x1 -> x0, blocking collectives: 3.84 us -> none  [corner_turn(): lax.all_to_all(lax.all_to_all(spectrum, 'wide', split_axis=1, concat_axis...]
  transfers between devices with their start and end apart: 1 -> 0, of which waited for: 1 -> 0; matrix products, arithmetic and copies ran while one was open for 0% -> 0% of each run, Pallas kernels for 0% -> 0%
where the time goes in v1:
time: 20.5 us; the launch traced here: 20.3 us
  Pallas kernels  18.9 us (92%)
  local copies, waits for them, and re-layouts  1.33 us (6%)
    pallas_call x1, Pallas kernels, transform(): pl.pallas_call(functools.partial(transform_kernel, n_wide, n_tm), out_sha...  16.1 us
    pallas_call x1, Pallas kernels, correlate(): pl.pallas_call(functools.partial(correlate_kernel, frames, chunk), out_sh...  2.78 us
    reshape x1, local copies, waits for them, and re-layouts, transform(): channels.reshape(count, 1)  1.33 us

profile of v1, /device:TPU:0, one launch (start us, length us, event | category | flops | bytes accessed | tf_op | source)
XLA Modules:
  0.0 20.3 jit_solution(15173509170630366192)
XLA Ops:
  0.0 1.3 %copy.4.channels_ref = s32[16,1]{1,0:T(8,128)} copy(s32[16,1]{0,1:T(1,128)} %bitcast.6) | data formatting | bytes 128 | tf_op jit(solution)/shard_map/reshape | solution.py:143
  1.3 16.1 %transform.1 = bf16[8,2,1,16,256]{4,3,2,1,0:T(8,128)(2,1)} custom-call(s32[16,1]{1,0:T(8,128)} %copy.4.channels_ref, bf16[256,16384]{1,0:T(8,128)(2,1)} %v_hbm.1), custom_call_target="tpu_custom_call" | custom-call | tf_op jit(solution)/shard_map/transform/pallas_call | solution.py:123
  17.5 2.8 %correlate.1 = bf16[128,64,128]{2,1,0:T(8,128)(2,1)} custom-call(s32[2,128]{1,0:T(2,128)} %bitcast.5, bf16[8,2,16,256]{3,2,1,0:T(8,128)(2,1)} %bitcast.4), custom_call_target="tpu_custom_call" | custom-call | tf_op jit(solution)/shard_map/correlate/pallas_call | solution.py:181

commit v2 on v1

--- a/solution.py
+++ b/solution.py
@@ -10,6 +10,12 @@
 TILE = 64
 NFFT = 2048
 LANES = 128
+SUBLANES = 8
+OUT = pltpu.HBM
+UNROLL = 16
+KSPLIT = 1
+GROUP = 2
+MAXCHUNKS = 1
 MESH = pl.DeviceIdType.MESH
 
 
@@ -20,10 +26,13 @@
 
 
 def fill_table(channels_ref, table):
-    count = channels_ref.shape[0]
+    count = channels_ref.shape[1]
     highs = NFFT // LANES
     scale = 1.0 / jnp.sqrt(jnp.float32(0.375 * NFFT))
-    channels = channels_ref[...]
+    square = (count, count)
+    diagonal = lax.broadcasted_iota(jnp.int32, square, 0) == lax.broadcasted_iota(jnp.int32, square, 1)
+    row = jnp.broadcast_to(channels_ref[...].astype(jnp.float32), square)
+    channels = jnp.sum(jnp.where(diagonal, row, 0.0), axis=1, keepdims=True).astype(jnp.int32)
     low = lax.broadcasted_iota(jnp.int32, (count, LANES), 1)
     low_cos, low_sin = cos_sin(channels, low)
     high_cos, high_sin = cos_sin(channels, LANES * low)
@@ -41,16 +50,33 @@
         table[:, columns] = jnp.concatenate([real, imag], 0).astype(jnp.bfloat16)
 
 
+def transformed(table, block):
+    half = NFFT // KSPLIT
+    return sum(
+        lax.dot_general(
+            table[:, k : k + half],
+            block[:, k : k + half],
+            (((1,), (1,)), ((), ())),
+            preferred_element_type=jnp.float32,
+        )
+        for k in range(0, NFFT, half)
+    )
+
+
 def transform_kernel(
-    n_wide, n_tm, channels_ref, v_hbm, out, blocks, table, staged, send, in_sems, send_sems, recv_sems, own_sem
+    n_wide, n_tm, channels_hbm, v_hbm, out, channels, blocks, table, staged, send, in_sems, send_sem, recv_sem
 ):
     frames, in_dev, _ = blocks.shape
-    count = channels_ref.shape[0]
-    rows = 2 * frames
+    chunks, count, rows, _ = send.shape
+    part = frames // chunks
+    group = GROUP if part % GROUP == 0 else 1
     wide, tm = lax.axis_index("wide"), lax.axis_index("tm")
     me = wide * n_tm + tm
     peers = n_wide * n_tm
-
+    per_dev = count // peers
+
+    fetch = pltpu.make_async_copy(channels_hbm, channels, in_sems.at[frames])
+    fetch.start()
     loads = [
         pltpu.make_async_copy(
             v_hbm.at[:, pl.ds(f * NFFT, NFFT)], blocks.at[f], in_sems.at[f]
@@ -60,58 +86,65 @@
     for load in loads:
         load.start()
 
+    def device(peer):
+        return {"wide": peer // n_tm, "tm": lax.rem(peer, n_tm)}
+
     barrier = pltpu.get_barrier_semaphore()
 
     def greet(k, carry):
         peer = lax.rem(me + k, peers)
-        pl.semaphore_signal(
-            barrier,
-            inc=1,
-            device_id={"wide": peer // n_tm, "tm": lax.rem(peer, n_tm)},
+        pl.semaphore_signal(barrier, inc=1, device_id=device(peer), device_id_type=MESH)
+        return carry
+
+    lax.fori_loop(1, peers, greet, 0)
+
+    fetch.wait()
+    fill_table(channels, table)
+
+    upper = 2 * wide // n_wide
+    own_turn = upper * me + (1 - upper) * (peers - 1 - me)
+
+    def peer_at(k):
+        turn = k + (k + peers - own_turn) // peers
+        return upper * turn + (1 - upper) * (peers - 1 - turn)
+
+    def copy_to(chunk, peer):
+        return pltpu.make_async_remote_copy(
+            src_ref=send.at[chunk, pl.ds(peer * per_dev, per_dev)],
+            dst_ref=out.at[wide, tm, chunk],
+            send_sem=send_sem,
+            recv_sem=recv_sem,
+            device_id=device(peer),
             device_id_type=MESH,
         )
-        return carry
-
-    lax.fori_loop(1, peers, greet, 0)
-
-    fill_table(channels_ref, table)
-
-    for f in range(frames):
-        loads[f].wait()
-        spectrum = lax.dot_general(
-            table[...], blocks[f], (((1,), (1,)), ((), ())), preferred_element_type=jnp.float32
-        )
-        for q in range(2):
-            staged[:, q * frames + f, :] = spectrum[q * count : (q + 1) * count]
-    send[...] = staged[...].astype(jnp.bfloat16)
-
-    pl.semaphore_wait(barrier, peers - 1)
-    per_dev = count // peers
-
-    def copy_to(k):
-        peer = lax.rem(me + k, peers)
-        return pltpu.make_async_remote_copy(
-            src_ref=send.at[pl.ds(peer * per_dev, per_dev)],
-            dst_ref=out.at[wide, tm],
-            send_sem=send_sems.at[k],
-            recv_sem=recv_sems.at[k],
-            device_id={"wide": peer // n_tm, "tm": lax.rem(peer, n_tm)},
-            device_id_type=MESH,
-        )
-
-    def start(k, carry):
-        copy_to(k).start()
-        return carry
-
-    def wait(k, carry):
-        copy_to(k).wait()
-        return carry
-
-    lax.fori_loop(1, peers, start, 0)
-    own = pltpu.make_async_copy(send.at[pl.ds(me * per_dev, per_dev)], out.at[wide, tm], own_sem)
-    own.start()
-    own.wait()
-    lax.fori_loop(1, peers, wait, 0)
+
+    for c in range(chunks):
+        for f0 in range(c * part, (c + 1) * part, group):
+            members = range(f0, f0 + group)
+            for f in members:
+                loads[f].wait()
+            spectrum = [transformed(table, blocks.at[f]) for f in members]
+            for f, values in zip(members, spectrum):
+                for q in range(2):
+                    staged[c, :, q * part + f - c * part, :] = values[q * count : (q + 1) * count]
+        send[c] = staged[c].astype(jnp.bfloat16)
+
+        if c == 0:
+            pl.semaphore_wait(barrier, peers - 1)
+
+        def start(k, carry):
+            copy_to(c, peer_at(k)).start()
+            return carry
+
+        lax.fori_loop(0, peers - 1, start, 0, unroll=peers <= UNROLL)
+        own = pltpu.make_async_copy(
+            send.at[c, pl.ds(me * per_dev, per_dev)], out.at[wide, tm, c], recv_sem
+        )
+        own.start()
+
+    others = send.at[:, pl.ds(0, (peers - 1) * per_dev)]
+    pltpu.make_async_copy(others, others, send_sem).wait()
+    pltpu.make_async_copy(send, send, recv_sem).wait()
 
 
 def transform(voltages, channels, n_wide, n_tm):
@@ -119,36 +152,34 @@
     frames = samples // NFFT
     count = channels.shape[0]
     peers = n_wide * n_tm
-    rows = 2 * frames
+    chunks = min(MAXCHUNKS, max(1, 2 * frames // SUBLANES))
+    rows = 2 * frames // chunks
     return pl.pallas_call(
         functools.partial(transform_kernel, n_wide, n_tm),
-        out_shape=jax.ShapeDtypeStruct((n_wide, n_tm, count // peers, rows, in_dev), jnp.bfloat16),
-        in_specs=[
-            pl.BlockSpec(memory_space=pltpu.VMEM),
-            pl.BlockSpec(memory_space=pltpu.HBM),
-        ],
-        out_specs=pl.BlockSpec(memory_space=pltpu.VMEM),
+        out_shape=jax.ShapeDtypeStruct((n_wide, n_tm, chunks, count // peers, rows, in_dev), jnp.bfloat16),
+        in_specs=[pl.BlockSpec(memory_space=pltpu.HBM)] * 2,
+        out_specs=pl.BlockSpec(memory_space=OUT),
         scratch_shapes=[
+            pltpu.VMEM((1, count), jnp.int32),
             pltpu.VMEM((frames, in_dev, NFFT), jnp.bfloat16),
             pltpu.VMEM((2 * count, NFFT), jnp.bfloat16),
-            pltpu.VMEM((count, rows, in_dev), jnp.float32),
-            pltpu.VMEM((count, rows, in_dev), jnp.bfloat16),
-            pltpu.SemaphoreType.DMA((frames,)),
-            pltpu.SemaphoreType.DMA((peers,)),
-            pltpu.SemaphoreType.DMA((peers,)),
+            pltpu.VMEM((chunks, count, rows, in_dev), jnp.float32),
+            pltpu.VMEM((chunks, count, rows, in_dev), jnp.bfloat16),
+            pltpu.SemaphoreType.DMA((frames + 1,)),
+            pltpu.SemaphoreType.DMA,
             pltpu.SemaphoreType.DMA,
         ],
         compiler_params=pltpu.CompilerParams(collective_id=0, has_side_effects=True),
         name="transform",
-    )(channels.reshape(count, 1), voltages)
+    )(channels.reshape(1, count), voltages)
 
 
 def correlate_kernel(frames, chunk, pairs_ref, spectra, out, left, right, products, sems):
-    groups, n_tm, rows, in_group = spectra.shape
+    groups, n_tm, chunks, rows, in_group = spectra.shape
     half = rows // 2
     npairs = out.shape[0]
     for g in range(groups):
-        blocks = [spectra[g, t].astype(jnp.float32) for t in range(n_tm)]
+        blocks = [spectra[g, t, c].astype(jnp.float32) for t in range(n_tm) for c in range(chunks)]
         plain = jnp.concatenate(blocks, 0)
         swapped = jnp.concatenate([x for b in blocks for x in (b[half:], -b[:half])], 0)
         left[g * in_group : (g + 1) * in_group, :] = plain.T.astype(jnp.bfloat16)
@@ -173,10 +204,10 @@
 
 
 def correlate(spectra, pairs, frames):
-    groups, n_tm, rows, in_group = spectra.shape
+    groups, n_tm, chunks, rows, in_group = spectra.shape
     npairs = pairs.shape[1]
     inputs = groups * in_group
-    depth = n_tm * rows
+    depth = n_tm * chunks * rows
     chunk = 16 if npairs % 16 == 0 else npairs
     return pl.pallas_call(
         functools.partial(correlate_kernel, frames, chunk),
@@ -205,10 +236,10 @@
     turned = transform(voltages, channels, n_wide, n_tm)
     visibility = []
     for s in range(per_dev):
-        spectra = turned[:, :, s]
+        spectra = turned[:, :, :, s]
         if in_dev % TILE:
-            rows = spectra.shape[2]
-            spectra = spectra.transpose(1, 2, 0, 3).reshape(1, n_tm, rows, n_wide * in_dev)
+            chunks, rows = spectra.shape[2:4]
+            spectra = spectra.transpose(1, 2, 3, 0, 4).reshape(1, n_tm, chunks, rows, n_wide * in_dev)
         visibility.append(correlate(spectra, tile_pairs.T, frames_all))
     return jnp.stack(visibility)
 

time: 20.5 us -> 15.4 us (0.75)
  Pallas kernels: 18.9 us -> 15.3 us
  local copies, waits for them, and re-layouts: 1.33 us -> 0 us
    pallas_call x1, Pallas kernels: 16.1 us -> 12.5 us  [transform(): pl.pallas_call(functools.partial(transform_kernel, n_wide, n_tm), out_sha...]
    reshape x1 -> x0, local copies, waits for them, and re-layouts: 1.33 us -> none  [transform(): channels.reshape(count, 1)]
where the time goes in v2:
time: 15.4 us; the launch traced here: 15.3 us
  Pallas kernels  15.3 us (99%)
    pallas_call x1, Pallas kernels, transform(): pl.pallas_call(functools.partial(transform_kernel, n_wide, n_tm), out_sha...  12.5 us
    pallas_call x1, Pallas kernels, correlate(): pl.pallas_call(functools.partial(correlate_kernel, frames, chunk), out_sh...  2.78 us

profile of v2, /device:TPU:0, one launch (start us, length us, event | category | flops | bytes accessed | tf_op | source)
XLA Modules:
  0.0 15.3 jit_solution(17329542512381876466)
XLA Ops:
  0.0 12.5 %transform.1 = bf16[8,2,1,1,16,256]{5,4,3,2,1,0:T(8,128)(2,1)} custom-call(s32[1,16]{1,0:T(1,128)} %bitcast.6, bf16[256,16384]{1,0:T(8,128)(2,1)} %v_hbm.1), custom_call_target="tpu_custom_call" | custom-call | tf_op jit(solution)/shard_map/transform/pallas_call | solution.py:157
  12.5 2.8 %correlate.1 = bf16[128,64,128]{2,1,0:T(8,128)(2,1)} custom-call(s32[2,128]{1,0:T(2,128)} %bitcast.5, bf16[8,2,1,16,256]{4,3,2,1,0:T(8,128)(2,1)} %bitcast.4), custom_call_target="tpu_custom_call" | custom-call | tf_op jit(solution)/shard_map/correlate/pallas_call | solution.py:212
